TPU v7x, 32 devices: a whole 2x2x4 slice. The times are simulated.
32 devices in a mesh: dp: 8 (over z, x), tensor: 4 (over y, core).
Axes of the slice: x: 2, y: 2, z: 4, core: 2. Of those that a mesh axis runs over, the one named last changes fastest.
Arguments:
- tokens: bfloat16 [8192, 768], P(('dp', 'tensor')), may hold values from -6 to 6
- cotangent: bfloat16 [8192, 768], P(('dp', 'tensor')), may hold values from -6 to 6
- prefix: int32 [8], P('dp'), may hold values from 102 to 512
- w_qkv: bfloat16 [2, 3, 768, 768], P(None, None, None, 'tensor'), may hold values from -0.3125 to 0.3125
- bias_qv: float32 [2, 2, 768], P(None, None, 'tensor'), may hold values from -1.8 to 1.8
- w_out: bfloat16 [2, 768, 768], P(None, 'tensor'), may hold values from -0.625 to 0.625
- bias_out: float32 [2, 768], replicated, may hold values from -1.8 to 1.8
- norm_gain: float32 [2, 2, 768], replicated, may hold values from 0.5 to 1.5
- norm_bias: float32 [2, 2, 768], replicated, may hold values from -1.8 to 1.8
- w_up: bfloat16 [2, 768, 3072], P(None, None, 'tensor'), may hold values from -0.21875 to 0.21875
- bias_up: float32 [2, 3072], P(None, 'tensor'), may hold values from -3 to 3
- w_down: bfloat16 [2, 3072, 768], P(None, 'tensor'), may hold values from -0.15625 to 0.15625
- bias_down: float32 [2, 768], replicated, may hold values from -1.8 to 1.8
Outputs:
- output: float32 [8192, 768], P(('dp', 'tensor'))
- grad_tokens: float32 [8192, 768], P(('dp', 'tensor'))
- grad_w_qkv: float32 [2, 3, 768, 768], P(None, None, 'dp', 'tensor')
- grad_bias_qv: float32 [2, 2, 768], P(None, None, 'tensor')
- grad_w_out: float32 [2, 768, 768], P(None, 'tensor', 'dp')
- grad_bias_out: float32 [2, 768], replicated
- grad_norm_gain: float32 [2, 2, 768], replicated
- grad_norm_bias: float32 [2, 2, 768], replicated
- grad_w_up: float32 [2, 768, 3072], P(None, 'dp', 'tensor')
- grad_bias_up: float32 [2, 3072], P(None, 'tensor')
- grad_w_down: float32 [2, 3072, 768], P(None, 'tensor', 'dp')
- grad_bias_down: float32 [2, 768], replicated
All inputs are finite; a program needn't handle non-finite values.
Results may differ from a plain program's by a relative error of at most 0.025.
The roundings to bfloat16 on the way count: a program that leaves them out, or rounds other values in their place, can miss the bound.
Values may be sent and summed in bfloat16 or wider, within the bound.
A program may use at most 192 MiB of HBM per device.

v0:
```python
import functools
import math
import jax
import jax.numpy as jnp
from jax import lax
from jax.sharding import PartitionSpec as P

HDIM = 64
LEN = 1024
MEM = 10
EPSILON = 1e-06
HIGHEST = lax.Precision.HIGHEST


def gather_rows(values_in):
    return lax.all_gather(values_in, "tensor", axis=0, tiled=True)


def sum_rows(term_fn, row_count):
    return lax.psum_scatter(
        term_fn(jnp.int32(0), lax.axis_size("tensor") * row_count),
        "tensor",
        scatter_dimension=0,
        tiled=True,
    )


def gather_grad(values_in):
    return lax.all_gather(values_in, "tensor", axis=0, tiled=True)


def sum_grad(term_fn, row_count):
    return lax.psum_scatter(
        term_fn(jnp.int32(0), lax.axis_size("tensor") * row_count),
        "tensor",
        scatter_dimension=0,
        tiled=True,
    )


def normalize(total, gain, shift):
    row_mean = jnp.mean(total, axis=-1, keepdims=True)
    centered = total - row_mean
    spread = jnp.mean(centered * centered, axis=-1, keepdims=True)
    recip = lax.rsqrt(spread + EPSILON)
    normal = centered * recip
    return (normal * gain + shift, normal, recip)


def normalize_back(grad_in, normal, recip, gain):
    scaled = grad_in * gain
    inner = (
        scaled
        - jnp.mean(scaled, axis=-1, keepdims=True)
        - normal * jnp.mean(scaled * normal, axis=-1, keepdims=True)
    )
    return (recip * inner, jnp.sum(grad_in * normal, axis=0), jnp.sum(grad_in, axis=0))


def probabilities(query_block, keys_seq, first_row, prefix_len):
    block_rows = query_block.shape[0]
    scale = 1.0 / math.sqrt(HDIM)
    scores = (
        jnp.einsum("bhd,khd->hbk", query_block, keys_seq, preferred_element_type=jnp.float32)
        * scale
    )
    row_pos = first_row + lax.broadcasted_iota(jnp.int32, (block_rows, LEN), 0)
    col_pos = lax.broadcasted_iota(jnp.int32, (block_rows, LEN), 1)
    visible = (
        (col_pos <= row_pos) | (col_pos < prefix_len) | (row_pos < MEM) | (row_pos >= LEN - MEM)
    )
    scores = jnp.where(visible[None], scores, -1e30)
    row_max = jnp.max(scores, axis=-1, keepdims=True)
    expo = jnp.exp(scores - row_max)
    return expo / jnp.sum(expo, axis=-1, keepdims=True)


def attention_forward(query, keys, values, prefix):
    seq_count = prefix.shape[0]
    width = query.shape[1]
    local_heads = width // HDIM
    block_rows = min(512, LEN)
    block_count = LEN // block_rows
    shape_four = (seq_count, LEN, local_heads, HDIM)

    def per_sequence(sequence):
        query_seq, keys_seq, values_seq, prefix_len = sequence

        def per_block(block_index):
            first_row = block_index * block_rows
            query_block = lax.dynamic_slice_in_dim(query_seq, first_row, block_rows, 0)
            probs = probabilities(query_block, keys_seq, first_row, prefix_len)
            return jnp.einsum(
                "hbk,khd->bhd",
                probs.astype(jnp.bfloat16),
                values_seq,
                preferred_element_type=jnp.float32,
            ).astype(jnp.bfloat16)

        blocks = lax.map(per_block, jnp.arange(block_count, dtype=jnp.int32))
        return blocks.reshape(LEN, local_heads, HDIM)

    context = lax.map(
        per_sequence,
        (query.reshape(shape_four), keys.reshape(shape_four), values.reshape(shape_four), prefix),
    )
    return context.reshape(seq_count * LEN, width)


def attention_backward(query, keys, values, grad_context, prefix):
    seq_count = prefix.shape[0]
    width = query.shape[1]
    local_heads = width // HDIM
    block_rows = min(512, LEN)
    block_count = LEN // block_rows
    scale = 1.0 / math.sqrt(HDIM)
    shape_four = (seq_count, LEN, local_heads, HDIM)

    def per_sequence(sequence):
        query_seq, keys_seq, values_seq, grad_seq, prefix_len = sequence

        def per_block(running, block_index):
            keys_acc, values_acc = running
            first_row = block_index * block_rows
            query_block = lax.dynamic_slice_in_dim(query_seq, first_row, block_rows, 0)
            grad_block = lax.dynamic_slice_in_dim(grad_seq, first_row, block_rows, 0)
            probs = probabilities(query_block, keys_seq, first_row, prefix_len)
            probs_low = probs.astype(jnp.bfloat16)
            grad_probs = jnp.einsum(
                "bhd,khd->hbk",
                grad_block,
                values_seq,
                precision=HIGHEST,
                preferred_element_type=jnp.float32,
            )
            grad_scores = probs * (grad_probs - jnp.sum(probs * grad_probs, axis=-1, keepdims=True))
            grad_query = (
                jnp.einsum(
                    "hbk,khd->bhd",
                    grad_scores,
                    keys_seq,
                    precision=HIGHEST,
                    preferred_element_type=jnp.float32,
                )
                * scale
            )
            keys_acc = (
                keys_acc
                + jnp.einsum(
                    "hbk,bhd->khd",
                    grad_scores,
                    query_block,
                    precision=HIGHEST,
                    preferred_element_type=jnp.float32,
                )
                * scale
            )
            values_acc = values_acc + jnp.einsum(
                "hbk,bhd->khd",
                probs_low,
                grad_block,
                precision=HIGHEST,
                preferred_element_type=jnp.float32,
            )
            return ((keys_acc, values_acc), grad_query)

        zero_acc = jnp.zeros((LEN, local_heads, HDIM), jnp.float32)
        (keys_acc, values_acc), grad_query = lax.scan(
            per_block, (zero_acc, zero_acc), jnp.arange(block_count, dtype=jnp.int32)
        )
        return (grad_query.reshape(LEN, local_heads, HDIM), keys_acc, values_acc)

    grad_q, grad_k, grad_v = lax.map(
        per_sequence,
        (
            query.reshape(shape_four),
            keys.reshape(shape_four),
            values.reshape(shape_four),
            grad_context.reshape(shape_four),
            prefix,
        ),
    )
    flat = (seq_count * LEN, width)
    return (grad_q.reshape(flat), grad_k.reshape(flat), grad_v.reshape(flat))


def local(
    tokens,
    cotangent,
    prefix,
    w_qkv,
    bias_qv,
    w_out,
    bias_out,
    norm_gain,
    norm_bias,
    w_up,
    bias_up,
    w_down,
    bias_down,
):
    my_rows = tokens.shape[0]
    layer_count = w_qkv.shape[0]
    state = tokens.astype(jnp.float32)
    stored = []
    for layer_index in range(layer_count):
        input_whole = gather_rows(state.astype(jnp.bfloat16))
        query = (
            jnp.dot(input_whole, w_qkv[layer_index, 0], preferred_element_type=jnp.float32)
            + bias_qv[layer_index, 0]
        ).astype(jnp.bfloat16)
        keys = jnp.dot(
            input_whole, w_qkv[layer_index, 1], preferred_element_type=jnp.float32
        ).astype(jnp.bfloat16)
        values = (
            jnp.dot(input_whole, w_qkv[layer_index, 2], preferred_element_type=jnp.float32)
            + bias_qv[layer_index, 1]
        ).astype(jnp.bfloat16)
        context = attention_forward(query, keys, values, prefix)

        def attn_term(row_start, row_count):
            return jnp.dot(context, w_out[layer_index], preferred_element_type=jnp.float32)

        attn_share = sum_rows(attn_term, my_rows)
        normed, normal_one, recip_one = normalize(
            state + attn_share + bias_out[layer_index],
            norm_gain[layer_index, 0],
            norm_bias[layer_index, 0],
        )
        normed_whole = gather_rows(normed.astype(jnp.bfloat16))
        hidden = (
            jnp.dot(normed_whole, w_up[layer_index], preferred_element_type=jnp.float32)
            + bias_up[layer_index]
        )
        active = jax.nn.gelu(hidden, approximate=False).astype(jnp.bfloat16)

        def ffn_term(row_start, row_count):
            return jnp.dot(active, w_down[layer_index], preferred_element_type=jnp.float32)

        ffn_share = sum_rows(ffn_term, my_rows)
        state, normal_two, recip_two = normalize(
            normed + ffn_share + bias_down[layer_index],
            norm_gain[layer_index, 1],
            norm_bias[layer_index, 1],
        )
        stored.append(
            (
                input_whole,
                query,
                keys,
                values,
                context,
                normal_one,
                recip_one,
                normed_whole,
                hidden,
                active,
                normal_two,
                recip_two,
            )
        )
    grad_state = cotangent.astype(jnp.float32)
    weight_grads = [None] * layer_count
    bias_grads = [None] * layer_count
    shared_grads = [None] * layer_count
    for layer_index in reversed(range(layer_count)):
        (
            input_whole,
            query,
            keys,
            values,
            context,
            normal_one,
            recip_one,
            normed_whole,
            hidden,
            active,
            normal_two,
            recip_two,
        ) = stored[layer_index]
        grad_two, gain_two, shift_two = normalize_back(
            grad_state, normal_two, recip_two, norm_gain[layer_index, 1]
        )
        ffn_grad_whole = gather_grad(grad_two.astype(jnp.bfloat16))
        grad_down = jnp.einsum(
            "rf,rd->fd", active, ffn_grad_whole, preferred_element_type=jnp.float32
        )
        grad_active = jnp.einsum(
            "rd,fd->rf", ffn_grad_whole, w_down[layer_index], preferred_element_type=jnp.float32
        )
        _, gelu_pull = jax.vjp(functools.partial(jax.nn.gelu, approximate=False), hidden)
        grad_hidden = gelu_pull(grad_active)[0]
        grad_up = jnp.einsum(
            "rd,rf->df",
            normed_whole,
            grad_hidden,
            precision=HIGHEST,
            preferred_element_type=jnp.float32,
        )
        grad_bias_up = jnp.sum(grad_hidden, axis=0)

        def ffn_back_term(row_start, row_count):
            return jnp.einsum(
                "rf,df->rd",
                grad_hidden,
                w_up[layer_index],
                precision=HIGHEST,
                preferred_element_type=jnp.float32,
            )

        grad_normed = sum_grad(ffn_back_term, my_rows) + grad_two
        grad_one, gain_one, shift_one = normalize_back(
            grad_normed, normal_one, recip_one, norm_gain[layer_index, 0]
        )
        attn_grad_whole = gather_grad(grad_one.astype(jnp.bfloat16))
        grad_out = jnp.einsum(
            "rh,rd->hd", context, attn_grad_whole, preferred_element_type=jnp.float32
        )
        grad_context = jnp.einsum(
            "rd,hd->rh", attn_grad_whole, w_out[layer_index], preferred_element_type=jnp.float32
        )
        grad_query, grad_keys, grad_values = attention_backward(
            query, keys, values, grad_context, prefix
        )
        grad_qkv = jnp.stack(
            [
                jnp.einsum(
                    "rd,rh->dh",
                    input_whole,
                    grad_query,
                    precision=HIGHEST,
                    preferred_element_type=jnp.float32,
                ),
                jnp.einsum(
                    "rd,rh->dh",
                    input_whole,
                    grad_keys,
                    precision=HIGHEST,
                    preferred_element_type=jnp.float32,
                ),
                jnp.einsum(
                    "rd,rh->dh",
                    input_whole,
                    grad_values,
                    precision=HIGHEST,
                    preferred_element_type=jnp.float32,
                ),
            ]
        )
        grad_bias_qv = jnp.stack([jnp.sum(grad_query, axis=0), jnp.sum(grad_values, axis=0)])

        def input_back_term(row_start, row_count):
            total = jnp.einsum(
                "rh,dh->rd",
                grad_query,
                w_qkv[layer_index, 0],
                precision=HIGHEST,
                preferred_element_type=jnp.float32,
            )
            total = total + jnp.einsum(
                "rh,dh->rd",
                grad_keys,
                w_qkv[layer_index, 1],
                precision=HIGHEST,
                preferred_element_type=jnp.float32,
            )
            return total + jnp.einsum(
                "rh,dh->rd",
                grad_values,
                w_qkv[layer_index, 2],
                precision=HIGHEST,
                preferred_element_type=jnp.float32,
            )

        grad_state = sum_grad(input_back_term, my_rows) + grad_one
        weight_grads[layer_index] = (grad_qkv, grad_out, grad_up, grad_down)
        bias_grads[layer_index] = (grad_bias_qv, grad_bias_up)
        shared_grads[layer_index] = (
            jnp.sum(grad_one, axis=0),
            jnp.stack([gain_one, gain_two]),
            jnp.stack([shift_one, shift_two]),
            jnp.sum(grad_two, axis=0),
        )
    stacked_weights = tuple(
        (
            jnp.stack([weight_grads[level][member] for level in range(layer_count)])
            for member in range(4)
        )
    )
    summed_qkv, summed_out, summed_up, summed_down = (
        lax.psum_scatter(stacked_weights[0], "dp", scatter_dimension=2, tiled=True),
        lax.psum_scatter(stacked_weights[1], "dp", scatter_dimension=2, tiled=True),
        lax.psum_scatter(stacked_weights[2], "dp", scatter_dimension=1, tiled=True),
        lax.psum_scatter(stacked_weights[3], "dp", scatter_dimension=2, tiled=True),
    )
    stacked_bias_qv = jnp.stack([bias_grads[level][0] for level in range(layer_count)])
    stacked_bias_up = jnp.stack([bias_grads[level][1] for level in range(layer_count)])
    summed_bias_qv, summed_bias_up = lax.psum((stacked_bias_qv, stacked_bias_up), "dp")
    stacked_shared = tuple(
        (
            jnp.stack([shared_grads[level][member] for level in range(layer_count)])
            for member in range(4)
        )
    )
    summed_bias_out, summed_gain, summed_shift, summed_bias_down = lax.psum(
        stacked_shared, ("dp", "tensor")
    )
    return (
        state,
        grad_state,
        summed_qkv,
        summed_bias_qv,
        summed_out,
        summed_bias_out,
        summed_gain,
        summed_shift,
        summed_up,
        summed_bias_up,
        summed_down,
        summed_bias_down,
    )


def solution(mesh):
    in_specs = (
        P(("dp", "tensor"), None),
        P(("dp", "tensor"), None),
        P("dp"),
        P(None, None, None, "tensor"),
        P(None, None, "tensor"),
        P(None, "tensor", None),
        P(),
        P(),
        P(),
        P(None, None, "tensor"),
        P(None, "tensor"),
        P(None, "tensor", None),
        P(),
    )
    out_specs = (
        P(("dp", "tensor"), None),
        P(("dp", "tensor"), None),
        P(None, None, "dp", "tensor"),
        P(None, None, "tensor"),
        P(None, "tensor", "dp"),
        P(),
        P(),
        P(),
        P(None, "dp", "tensor"),
        P(None, "tensor"),
        P(None, "tensor", "dp"),
        P(),
    )
    return jax.shard_map(local, mesh=mesh, in_specs=in_specs, out_specs=out_specs, check_vma=False)
```

profile of v0, /device:TPU:0, one launch (start us, length us, event | category | flops | bytes accessed | tf_op | source)
XLA Modules:
  0.0 1125.7 jit_solution(9122916788855121678)
XLA Ops:
  8.7 23.2 %all-gather.9.cloned.1.call-done = bf16[1024,768]{1,0:T(8,128)(2,1)} async-done(((bf16[256,768]{1,0:T(8,128)(2,1)}), bf16[1024,768]{1,0:T(8,128)(2,1)}) %all-gather.9.cloned.1.call-update) | async-done | bytes 1572880 | tf_op jit(solution)/shard_map/all_gather | solution.py:16
  38.0 23.0 %while.86 = (s32[]{:T(128)}, bf16[2,512,3,64]{1,3,2,0:T(8,128)(2,1)S(1)}, s32[2]{0:T(128)S(1)}, s32[]{:T(128)}, bf16[1024,3,64]{0,2,1:T(8,128)(2,1)S(1)}, /*inde...) while((s32[]{:T(128)}, ...), condition=%wide.region_3.4_spmd, body=%wide.region_0.3_spmd.sunk | while | flops 414289920 | bytes 14833859 | solution.py:100
  65.6 37.9 %reduce-scatter.16.cloned.1.call-done = f32[256,768]{1,0:T(8,128)} async-done(((f32[1024,768]{1,0:T(8,128)}), f32[256,768]{1,0:T(8,128)}) %reduce-scatter.16.cloned.1.call-update) | async-done | bytes 786448 | tf_op jit(solution)/shard_map/reduce_scatter | solution.py:20
  106.6 19.2 %all-gather.11.cloned.1.call-done = bf16[1024,768]{1,0:T(8,128)(2,1)} async-done(((bf16[256,768]{1,0:T(8,128)(2,1)}), bf16[1024,768]{1,0:T(8,128)(2,1)}) %all-gather.11.cloned.1.call-update) | async-done | bytes 1572880 | tf_op jit(solution)/shard_map/all_gather | solution.py:16
  142.4 37.4 %reduce-scatter.18.cloned.1.call-done = f32[256,768]{1,0:T(8,128)} async-done(((f32[1024,768]{1,0:T(8,128)}), f32[256,768]{1,0:T(8,128)}) %reduce-scatter.18.cloned.1.call-update) | async-done | bytes 786448 | tf_op jit(solution)/shard_map/reduce_scatter | solution.py:20
  182.6 19.8 %all-gather.13.cloned.1.call-done = bf16[1024,768]{1,0:T(8,128)(2,1)} async-done(((bf16[256,768]{1,0:T(8,128)(2,1)}), bf16[1024,768]{1,0:T(8,128)(2,1)}) %all-gather.13.cloned.1.call-update) | async-done | bytes 1572880 | tf_op jit(solution)/shard_map/all_gather | solution.py:16
  209.2 24.9 %while.87 = (s32[]{:T(128)}, bf16[2,512,3,64]{1,3,2,0:T(8,128)(2,1)S(1)}, s32[2]{0:T(128)S(1)}, s32[]{:T(128)}, bf16[1024,3,64]{0,2,1:T(8,128)(2,1)}, /*index=5*...) while((s32[]{:T(128)}, ...), condition=%wide.region_13.14_spmd, body=%wide.region_10.13_spmd.sunk | while | flops 414289920 | bytes 14833859 | solution.py:100
  237.8 37.8 %reduce-scatter.20.cloned.1.call-done = f32[256,768]{1,0:T(8,128)} async-done(((f32[1024,768]{1,0:T(8,128)}), f32[256,768]{1,0:T(8,128)}) %reduce-scatter.20.cloned.1.call-update) | async-done | bytes 786448 | tf_op jit(solution)/shard_map/reduce_scatter | solution.py:20
  278.4 19.8 %all-gather.15.cloned.1.call-done = bf16[1024,768]{1,0:T(8,128)(2,1)} async-done(((bf16[256,768]{1,0:T(8,128)(2,1)}), bf16[1024,768]{1,0:T(8,128)(2,1)}) %all-gather.15.cloned.1.call-update) | async-done | bytes 1572880 | tf_op jit(solution)/shard_map/all_gather | solution.py:16
  314.0 38.0 %reduce-scatter.22.cloned.1.call-done = f32[256,768]{1,0:T(8,128)} async-done(((f32[1024,768]{1,0:T(8,128)}), f32[256,768]{1,0:T(8,128)}) %reduce-scatter.22.cloned.1.call-update) | async-done | bytes 786448 | tf_op jit(solution)/shard_map/reduce_scatter | solution.py:20
  357.4 19.8 %all-gather.17.cloned.1.call-done = bf16[1024,768]{1,0:T(8,128)(2,1)} async-done(((bf16[256,768]{1,0:T(8,128)(2,1)}), bf16[1024,768]{1,0:T(8,128)(2,1)}) %all-gather.17.cloned.1.call-update) | async-done | bytes 1572880 | tf_op jit(solution)/shard_map/all_gather | solution.py:29
  391.3 38.1 %reduce-scatter.24.cloned.1.call-done = f32[256,768]{1,0:T(8,128)} async-done(((f32[1024,768]{1,0:T(8,128)}), f32[256,768]{1,0:T(8,128)}) %reduce-scatter.24.cloned.1.call-update) | async-done | bytes 786448 | tf_op jit(solution)/shard_map/reduce_scatter | solution.py:33
  435.2 18.8 %all-gather.19.cloned.1.call-done = bf16[1024,768]{1,0:T(8,128)(2,1)} async-done(((bf16[256,768]{1,0:T(8,128)(2,1)}), bf16[1024,768]{1,0:T(8,128)(2,1)}) %all-gather.19.cloned.1.call-update) | async-done | bytes 1572880 | tf_op jit(solution)/shard_map/all_gather | solution.py:29
  457.0 51.1 %while.88 = (s32[]{:T(128)}, f32[1024,3,64]{0,2,1:T(8,128)S(1)}, f32[1024,3,64]{0,2,1:T(8,128)S(1)}, f32[2,512,3,64]{1,3,2,0:T(8,128)S(1)}, s32[2]{0:T(128)S(1)}...) while((s32[]{:T(128)}, f32[1024,3,64]{0,2,1:T(8,128)S(1)}, ...), condition=%wide.region_29.30_spmd.clone, body=%wide.region_25.29_spmd.clone.sunk | while | flops 5059938816 | bytes 90376584 | solution.py:168
  518.0 38.0 %reduce-scatter.26.cloned.1.call-done = f32[256,768]{1,0:T(8,128)} async-done(((f32[1024,768]{1,0:T(8,128)}), f32[256,768]{1,0:T(8,128)}) %reduce-scatter.26.cloned.1.call-update) | async-done | bytes 786448 | tf_op jit(solution)/shard_map/reduce_scatter | solution.py:33
  560.1 19.6 %all-gather.21.cloned.1.call-done = bf16[1024,768]{1,0:T(8,128)(2,1)} async-done(((bf16[256,768]{1,0:T(8,128)(2,1)}), bf16[1024,768]{1,0:T(8,128)(2,1)}) %all-gather.21.cloned.1.call-update) | async-done | bytes 1572880 | tf_op jit(solution)/shard_map/all_gather | solution.py:29
  593.8 38.1 %reduce-scatter.28.cloned.1.call-done = f32[256,768]{1,0:T(8,128)} async-done(((f32[1024,768]{1,0:T(8,128)}), f32[256,768]{1,0:T(8,128)}) %reduce-scatter.28.cloned.1.call-update) | async-done | bytes 786448 | tf_op jit(solution)/shard_map/reduce_scatter | solution.py:33
  669.2 50.8 %while.89 = (s32[]{:T(128)}, f32[1024,3,64]{0,2,1:T(8,128)}, f32[1024,3,64]{0,2,1:T(8,128)S(1)}, f32[2,512,3,64]{1,3,2,0:T(8,128)S(1)}, s32[2]{0:T(128)S(1)}, /*...) while((s32[]{:T(128)}, f32[1024,3,64]{0,2,1:T(8,128)}, ...), condition=%wide.region_40.41_spmd.clone, body=%wide.region_36.40_spmd.clone.sunk | while | flops 5059938816 | bytes 95097240 | solution.py:168
  768.5 61.6 %all-reduce.5.cloned.1.call-done = f32[2,768,768]{1,0,2:T(2,128)} async-done(((f32[2,768,768]{1,0,2:T(2,128)}), f32[2,768,768]{1,0,2:T(2,128)}) %all-reduce.5.cloned.1.call-update) | async-done | bytes 4718608
  832.2 40.7 %all-reduce.1 = (f32[2,768]{1,0:T(2,128)}, f32[2,2,768]{2,1,0:T(2,128)}, f32[2,2,768]{2,1,0:T(2,128)}, f32[2,768]{1,0:T(2,128)}) all-reduce(f32[2,768]{1,0:T(2,128)S(1)} %pad_maximum_fusion.6, f32[2,2,768]{2,1,0:T(2,128)S(1)} %pad_maximum_fusion.4, ...), channel_id=1, replica_groups=mesh['dp'=8,'tensor'=4] {'dp','tensor'}, use_global_device_ids=true, to_apply=%region_51.52 | all-reduce | flops 9216 | bytes 73728 | tf_op jit(solution)/shard_map/psum | solution.py:405
  873.3 36.8 %all-reduce.2 = (f32[2,2,192]{2,1,0:T(2,128)}, f32[2,768]{1,0:T(2,128)}) all-reduce(f32[2,2,192]{2,1,0:T(2,128)S(1)} %pad_maximum_fusion.9, f32[2,768]{1,0:T(2,128)S(1)} %pad_maximum_fusion.7), channel_id=1, replica_groups=mesh['dp'=8,'tensor'=4] {'dp'}, use_global_device_ids=true, to_apply=%region_47.48 | all-reduce | flops 2304 | bytes 18432 | tf_op jit(solution)/shard_map/psum | solution.py:398
  912.0 24.5 %reduce-scatter.30.cloned.1.call-done = f32[256,768]{1,0:T(8,128)} async-done(((f32[1024,768]{1,0:T(8,128)}), f32[256,768]{1,0:T(8,128)}) %reduce-scatter.30.cloned.1.call-update) | async-done | bytes 786448 | tf_op jit(solution)/shard_map/reduce_scatter | solution.py:33
  938.7 80.7 %reduce-scatter.34.cloned.1.call-done = f32[96,1152]{1,0:T(8,128)} async-done(((f32[768,1152]{1,0:T(8,128)}), f32[96,1152]{1,0:T(8,128)}) %reduce-scatter.34.cloned.1.call-update) | async-done | bytes 442384
  1021.9 96.7 %reduce-scatter.32.cloned.1.call-done = f32[2,96,768]{2,1,0:T(8,128)} async-done(((f32[2,768,768]{2,1,0:T(8,128)}), f32[2,96,768]{2,1,0:T(8,128)}) %reduce-scatter.32.cloned.1.call-update) | async-done | bytes 589840 | tf_op jit(solution)/shard_map/reduce_scatter | solution.py:393
  (496 shorter events, 355.8 us)
Async XLA Ops:
  7.2 24.8 %all-gather.9.cloned.1.call-start = ((), (), s32[]{:S(2)}) async-start(), calls=%async_computation.11 | async-start | bytes 1966080 | tf_op jit(solution)/shard_map/all_gather | solution.py:16
  7.9 95.5 %reduce-scatter.16.cloned.1.call-start = ((), (), s32[]{:S(2)}) async-start(), calls=%async_computation.12 | async-start | bytes 3932160 | tf_op jit(solution)/shard_map/reduce_scatter | solution.py:20
  65.4 60.4 %all-gather.11.cloned.1.call-start = ((), (), s32[]{:S(2)}) async-start(), calls=%async_computation.13 | async-start | bytes 1966080 | tf_op jit(solution)/shard_map/all_gather | solution.py:16
  65.5 114.3 %copy-start.50 = (f32[768]{0:T(1024)}, f32[768]{0:T(1024)S(1)}, u32[]{:S(2)}) copy-start(f32[768]{0:T(1024)S(1)} %get-tuple-element.555) | copy-start | bytes 9220
  65.6 210.1 %copy-start.52 = (f32[768]{0:T(1024)}, f32[768]{0:T(1024)S(1)}, u32[]{:S(2)}) copy-start(f32[768]{0:T(1024)S(1)} %get-tuple-element.556) | copy-start | bytes 9220
  106.0 73.9 %reduce-scatter.18.cloned.1.call-start = ((), (), s32[]{:S(2)}) async-start(), calls=%async_computation.14 | async-start | bytes 3932160 | tf_op jit(solution)/shard_map/reduce_scatter | solution.py:20
  141.7 60.7 %all-gather.13.cloned.1.call-start = ((), (), s32[]{:S(2)}) async-start(), calls=%async_computation.15 | async-start | bytes 1966080 | tf_op jit(solution)/shard_map/all_gather | solution.py:16
  182.6 93.1 %reduce-scatter.20.cloned.1.call-start = ((), (), s32[]{:S(2)}) async-start(), calls=%async_computation.16 | async-start | bytes 3932160 | tf_op jit(solution)/shard_map/reduce_scatter | solution.py:20
  237.6 60.6 %all-gather.15.cloned.1.call-start = ((), (), s32[]{:S(2)}) async-start(), calls=%async_computation.17 | async-start | bytes 1966080 | tf_op jit(solution)/shard_map/all_gather | solution.py:16
  278.4 73.7 %reduce-scatter.22.cloned.1.call-start = ((), (), s32[]{:S(2)}) async-start(), calls=%async_computation.18 | async-start | bytes 3932160 | tf_op jit(solution)/shard_map/reduce_scatter | solution.py:20
  314.0 63.2 %all-gather.17.cloned.1.call-start = ((), (), s32[]{:S(2)}) async-start(), calls=%async_computation.19 | async-start | bytes 1966080 | tf_op jit(solution)/shard_map/all_gather | solution.py:29
  357.4 72.0 %reduce-scatter.24.cloned.1.call-start = ((), (), s32[]{:S(2)}) async-start(), calls=%async_computation.20 | async-start | bytes 3932160 | tf_op jit(solution)/shard_map/reduce_scatter | solution.py:33
  391.2 62.7 %all-gather.19.cloned.1.call-start = ((), (), s32[]{:S(2)}) async-start(), calls=%async_computation.21 | async-start | bytes 1966080 | tf_op jit(solution)/shard_map/all_gather | solution.py:29
  434.1 121.9 %reduce-scatter.26.cloned.1.call-start = ((), (), s32[]{:S(2)}) async-start(), calls=%async_computation.22 | async-start | bytes 3932160 | tf_op jit(solution)/shard_map/reduce_scatter | solution.py:33
  517.9 61.8 %all-gather.21.cloned.1.call-start = ((), (), s32[]{:S(2)}) async-start(), calls=%async_computation.23 | async-start | bytes 1966080 | tf_op jit(solution)/shard_map/all_gather | solution.py:29
  559.9 72.0 %reduce-scatter.28.cloned.1.call-start = ((), (), s32[]{:S(2)}) async-start(), calls=%async_computation.24 | async-start | bytes 3932160 | tf_op jit(solution)/shard_map/reduce_scatter | solution.py:33
  593.8 62.7 %all-gather.23.cloned.1.call-start = ((), (), s32[]{:S(2)}) async-start(), calls=%async_computation.25 | async-start | bytes 1966080 | tf_op jit(solution)/shard_map/all_gather | solution.py:29
  636.7 193.4 %all-reduce.5.cloned.1.call-start = ((), (), s32[]{:S(2)}) async-start(), calls=%async_computation.30 | async-start | bytes 9437184
  651.9 258.2 %reduce-scatter.36.cloned.1.call-start = ((), (), s32[]{:S(2)}) async-start(), calls=%async_computation.29 | async-start | bytes 1327104
  667.4 269.2 %reduce-scatter.30.cloned.1.call-start = ((), (), s32[]{:S(2)}) async-start(), calls=%async_computation.26 | async-start | bytes 3932160 | tf_op jit(solution)/shard_map/reduce_scatter | solution.py:33
  729.5 289.8 %reduce-scatter.34.cloned.1.call-start = ((), (), s32[]{:S(2)}) async-start(), calls=%async_computation.28 | async-start | bytes 3981312
  751.6 367.0 %reduce-scatter.32.cloned.1.call-start = ((), (), s32[]{:S(2)}) async-start(), calls=%async_computation.27 | async-start | bytes 5308416 | tf_op jit(solution)/shard_map/reduce_scatter | solution.py:393
  766.0 107.1 %copy-start.12 = (f32[1024,3,64]{0,2,1:T(8,128)S(1)}, f32[1024,3,64]{0,2,1:T(8,128)}, u32[]{:S(2)}) copy-start(f32[1024,3,64]{0,2,1:T(8,128)} %copy-done.10) | copy-start | bytes 2359300
  768.0 168.5 %copy-start.21 = (f32[256,768]{1,0:T(8,128)S(1)}, f32[256,768]{1,0:T(8,128)}, u32[]{:S(2)}) copy-start(f32[256,768]{1,0:T(8,128)} %copy-done.20) | copy-start | bytes 2359300
  (112 other events, 1739.2 us)
Sparse Core Ops, SparseCore 0:
  9.6 22.3 all-gather.8
  65.5 37.9 reduce-scatter.15
  106.1 19.6 all-gather.10
  141.9 37.9 reduce-scatter.17
  182.7 19.6 all-gather.12
  237.7 37.9 reduce-scatter.19
  278.5 19.6 all-gather.14
  314.1 37.9 reduce-scatter.21
  357.5 19.6 all-gather.16
  391.4 37.9 reduce-scatter.23
  434.2 19.6 all-gather.18
  518.0 37.9 reduce-scatter.25
  560.0 19.6 all-gather.20
  593.9 37.9 reduce-scatter.27
  636.8 19.6 all-gather.22
  660.4 169.6 all-reduce.4
  833.7 63.2 reduce-scatter.35
  899.5 36.9 reduce-scatter.29
  940.2 79.0 reduce-scatter.33
  1023.4 95.1 reduce-scatter.31
where the time goes:
time: 1130 us
  waiting for transfers between devices  672 us (59%)
  matrix products  242 us (21%)
  blocking collectives  77.5 us (7%)
  local copies, waits for them, and re-layouts  63.6 us (6%)
  other arithmetic  45.1 us (4%)
  between operations  16.6 us (1%)
    reduce_scatter x4, waiting for transfers between devices, sum_rows(): lax.psum_scatter(term_fn(jnp.int32(0), lax.axis_size('tensor') * row_coun...  151 us
    unnamed x23, waiting for transfers between devices  143 us
    reduce_scatter x4, waiting for transfers between devices, sum_grad(): lax.psum_scatter(term_fn(jnp.int32(0), lax.axis_size('tensor') * row_coun...  139 us
    reduce_scatter x1, waiting for transfers between devices, local(): lax.psum_scatter(stacked_weights[2], 'dp', scatter_dimension=1, tiled=True)  96.7 us
    all_gather x4, waiting for transfers between devices, gather_rows(): return lax.all_gather(values_in, 'tensor', axis=0, tiled=True)  82 us
    all_gather x4, waiting for transfers between devices, gather_grad(): return lax.all_gather(values_in, 'tensor', axis=0, tiled=True)  60 us
    unnamed x203, local copies, waits for them, and re-layouts  46.1 us
    sub x8, matrix products, probabilities(): expo = jnp.exp(scores - row_max)  45.9 us
  transfers between devices with their start and end apart: 20, of which 19 were waited for; matrix products, arithmetic and copies ran while one was open for 12% of the time, Pallas kernels for 0%

commit v1 on v0

--- a/solution.py
+++ b/solution.py
@@ -4,6 +4,7 @@
 import jax.numpy as jnp
 from jax import lax
 from jax.sharding import PartitionSpec as P
+from jax.lax import axis_index, axis_size, ppermute
 
 HDIM = 64
 LEN = 1024
@@ -12,8 +13,23 @@
 HIGHEST = lax.Precision.HIGHEST
 
 
+def watch_page(xs, k_dim):
+    small = axis_size("tensor")
+    carry_out, prior, state_now = (small, axis_index("tensor"), xs.shape[k_dim])
+    big, w1 = (xs, 1)
+    while w1 < carry_out:
+        mat_out = range(carry_out)
+        latest = map(lambda ii: (ii, (ii - w1) % carry_out), mat_out)
+        parts_out = list(latest)
+        low = ppermute(big, axis_name="tensor", perm=parts_out)
+        big = jnp.concatenate([big, low], axis=k_dim)
+        w1 = 2 * w1
+    out_arr = jnp.roll(big, prior * state_now, axis=k_dim)
+    return out_arr
+
+
 def gather_rows(values_in):
-    return lax.all_gather(values_in, "tensor", axis=0, tiled=True)
+    return watch_page(values_in, 0)
 
 
 def sum_rows(term_fn, row_count):

time: 1130 us -> 1170 us (1.035)
  waiting for transfers between devices: 672 us -> 691 us
  other arithmetic: 45.1 us -> 63.6 us
    ppermute x0 -> x8, waiting for transfers between devices: none -> 95.2 us  [watch_page(): low = ppermute(big, axis_name='tensor', perm=parts_out)]
    all_gather x4 -> x0, waiting for transfers between devices: 82 us -> none  [gather_rows(): return lax.all_gather(values_in, 'tensor', axis=0, tiled=True)]
    concatenate x0 -> x8, other arithmetic: none -> 21.8 us  [the longest x4 20.6 us: watch_page(): out_arr = jnp.roll(big, prior * state_now, axis=k_dim)]
    unnamed x203 -> x211, local copies, waits for them, and re-layouts: 46.1 us -> 43.8 us
    unnamed x23 -> x19, waiting for transfers between devices: 143 us -> 144 us
  transfers between devices with their start and end apart: 20 -> 24, of which waited for: 19 -> 23; matrix products, arithmetic and copies ran while one was open for 12% -> 11% of each run, Pallas kernels for 0% -> 0%
where the time goes in v1:
time: 1170 us; the launch traced here: 1160 us
  waiting for transfers between devices  691 us (59%)
  matrix products  235 us (20%)
  blocking collectives  77.5 us (7%)
  other arithmetic  63.6 us (5%)
  local copies, waits for them, and re-layouts  61.6 us (5%)
  between operations  16.4 us (1%)
    reduce_scatter x4, waiting for transfers between devices, sum_rows(): lax.psum_scatter(term_fn(jnp.int32(0), lax.axis_size('tensor') * row_coun...  156 us
    unnamed x19, waiting for transfers between devices  144 us
    reduce_scatter x4, waiting for transfers between devices, sum_grad(): lax.psum_scatter(term_fn(jnp.int32(0), lax.axis_size('tensor') * row_coun...  139 us
    reduce_scatter x1, waiting for transfers between devices, local(): lax.psum_scatter(stacked_weights[2], 'dp', scatter_dimension=1, tiled=True)  96.8 us
    ppermute x8, waiting for transfers between devices, watch_page(): low = ppermute(big, axis_name='tensor', perm=parts_out)  95.2 us
    all_gather x4, waiting for transfers between devices, gather_grad(): return lax.all_gather(values_in, 'tensor', axis=0, tiled=True)  59.5 us
    sub x8, matrix products, probabilities(): expo = jnp.exp(scores - row_max)  47.9 us
    unnamed x211, local copies, waits for them, and re-layouts  43.8 us
  transfers between devices with their start and end apart: 24, of which 23 were waited for; matrix products, arithmetic and copies ran while one was open for 11% of the time, Pallas kernels for 0%

profile of v1, /device:TPU:0, one launch (start us, length us, event | category | flops | bytes accessed | tf_op | source)
XLA Modules:
  0.0 1162.1 jit_solution(8466695938273648285)
XLA Ops:
  17.8 19.0 %collective-permute-done.1 = bf16[512,768]{1,0:T(8,128)(2,1)} collective-permute-done((bf16[512,768]{1,0:T(8,128)(2,1)S(1)}, bf16[512,768]{1,0:T(8,128)(2,1)}, u32[]{:S(2)}, u32[]{:S(2)}) %collective-permute-start.1) | collective-permute-done | bytes 786464 | tf_op jit(solution)/shard_map/ppermute | solution.py:24
  44.3 24.8 %while.86 = (s32[]{:T(128)}, bf16[2,512,3,64]{1,3,2,0:T(8,128)(2,1)S(1)}, s32[2]{0:T(128)S(1)}, s32[]{:T(128)}, bf16[1024,3,64]{0,2,1:T(8,128)(2,1)}, /*index=5*...) while((s32[]{:T(128)}, ...), condition=%wide.region_3.5_spmd, body=%wide.region_0.4_spmd.sunk | while | flops 414289920 | bytes 14833859 | solution.py:116
  72.9 38.2 %reduce-scatter.16.cloned.1.call-done = f32[256,768]{1,0:T(8,128)} async-done(((f32[1024,768]{1,0:T(8,128)}), f32[256,768]{1,0:T(8,128)}) %reduce-scatter.16.cloned.1.call-update) | async-done | bytes 786448 | tf_op jit(solution)/shard_map/reduce_scatter | solution.py:36
  120.1 18.2 %collective-permute-done.3 = bf16[512,768]{1,0:T(8,128)(2,1)S(1)} collective-permute-done((bf16[512,768]{1,0:T(8,128)(2,1)S(1)}, bf16[512,768]{1,0:T(8,128)(2,1)S(1)}, u32[]{:S(2)}, u32[]{:S(2)}) %collective-permute-start.3) | collective-permute-done | bytes 786464 | tf_op jit(solution)/shard_map/ppermute | solution.py:24
  157.8 38.9 %reduce-scatter.18.cloned.1.call-done = f32[256,768]{1,0:T(8,128)} async-done(((f32[1024,768]{1,0:T(8,128)}), f32[256,768]{1,0:T(8,128)}) %reduce-scatter.18.cloned.1.call-update) | async-done | bytes 786448 | tf_op jit(solution)/shard_map/reduce_scatter | solution.py:36
  205.8 18.4 %collective-permute-done.5 = bf16[512,768]{1,0:T(8,128)(2,1)} collective-permute-done((bf16[512,768]{1,0:T(8,128)(2,1)S(1)}, bf16[512,768]{1,0:T(8,128)(2,1)}, u32[]{:S(2)}, u32[]{:S(2)}) %collective-permute-start.5) | collective-permute-done | bytes 786464 | tf_op jit(solution)/shard_map/ppermute | solution.py:24
  235.4 24.9 %while.87 = (s32[]{:T(128)}, bf16[2,512,3,64]{1,3,2,0:T(8,128)(2,1)S(1)}, s32[2]{0:T(128)S(1)}, s32[]{:T(128)}, bf16[1024,3,64]{0,2,1:T(8,128)(2,1)}, /*index=5*...) while((s32[]{:T(128)}, ...), condition=%wide.region_13.15_spmd, body=%wide.region_10.14_spmd.sunk | while | flops 414289920 | bytes 14833859 | solution.py:116
  263.9 39.5 %reduce-scatter.20.cloned.1.call-done = f32[256,768]{1,0:T(8,128)} async-done(((f32[1024,768]{1,0:T(8,128)}), f32[256,768]{1,0:T(8,128)}) %reduce-scatter.20.cloned.1.call-update) | async-done | bytes 786448 | tf_op jit(solution)/shard_map/reduce_scatter | solution.py:36
  312.7 18.2 %collective-permute-done.7 = bf16[512,768]{1,0:T(8,128)(2,1)S(1)} collective-permute-done((bf16[512,768]{1,0:T(8,128)(2,1)S(1)}, bf16[512,768]{1,0:T(8,128)(2,1)S(1)}, u32[]{:S(2)}, u32[]{:S(2)}) %collective-permute-start.7) | collective-permute-done | bytes 786464 | tf_op jit(solution)/shard_map/ppermute | solution.py:24
  349.7 39.6 %reduce-scatter.22.cloned.1.call-done = f32[256,768]{1,0:T(8,128)} async-done(((f32[1024,768]{1,0:T(8,128)}), f32[256,768]{1,0:T(8,128)}) %reduce-scatter.22.cloned.1.call-update) | async-done | bytes 786448 | tf_op jit(solution)/shard_map/reduce_scatter | solution.py:36
  394.8 19.6 %all-gather.5.cloned.1.call-done = bf16[1024,768]{1,0:T(8,128)(2,1)} async-done(((bf16[256,768]{1,0:T(8,128)(2,1)}), bf16[1024,768]{1,0:T(8,128)(2,1)}) %all-gather.5.cloned.1.call-update) | async-done | bytes 1572880 | tf_op jit(solution)/shard_map/all_gather | solution.py:45
  428.5 38.1 %reduce-scatter.24.cloned.1.call-done = f32[256,768]{1,0:T(8,128)} async-done(((f32[1024,768]{1,0:T(8,128)}), f32[256,768]{1,0:T(8,128)}) %reduce-scatter.24.cloned.1.call-update) | async-done | bytes 786448 | tf_op jit(solution)/shard_map/reduce_scatter | solution.py:49
  472.4 18.8 %all-gather.7.cloned.1.call-done = bf16[1024,768]{1,0:T(8,128)(2,1)} async-done(((bf16[256,768]{1,0:T(8,128)(2,1)}), bf16[1024,768]{1,0:T(8,128)(2,1)}) %all-gather.7.cloned.1.call-update) | async-done | bytes 1572880 | tf_op jit(solution)/shard_map/all_gather | solution.py:45
  494.2 50.8 %while.88 = (s32[]{:T(128)}, f32[1024,3,64]{0,2,1:T(8,128)S(1)}, f32[1024,3,64]{0,2,1:T(8,128)S(1)}, f32[2,512,3,64]{1,3,2,0:T(8,128)S(1)}, s32[2]{0:T(128)S(1)}...) while((s32[]{:T(128)}, f32[1024,3,64]{0,2,1:T(8,128)S(1)}, ...), condition=%wide.region_29.31_spmd.clone, body=%wide.region_25.30_spmd.clone.sunk | while | flops 5059938816 | bytes 90376584 | solution.py:184
  554.9 38.0 %reduce-scatter.26.cloned.1.call-done = f32[256,768]{1,0:T(8,128)} async-done(((f32[1024,768]{1,0:T(8,128)}), f32[256,768]{1,0:T(8,128)}) %reduce-scatter.26.cloned.1.call-update) | async-done | bytes 786448 | tf_op jit(solution)/shard_map/reduce_scatter | solution.py:49
  597.3 19.3 %all-gather.9.cloned.1.call-done = bf16[1024,768]{1,0:T(8,128)(2,1)} async-done(((bf16[256,768]{1,0:T(8,128)(2,1)}), bf16[1024,768]{1,0:T(8,128)(2,1)}) %all-gather.9.cloned.1.call-update) | async-done | bytes 1572880 | tf_op jit(solution)/shard_map/all_gather | solution.py:45
  630.7 38.1 %reduce-scatter.28.cloned.1.call-done = f32[256,768]{1,0:T(8,128)} async-done(((f32[1024,768]{1,0:T(8,128)}), f32[256,768]{1,0:T(8,128)}) %reduce-scatter.28.cloned.1.call-update) | async-done | bytes 786448 | tf_op jit(solution)/shard_map/reduce_scatter | solution.py:49
  703.7 51.1 %while.89 = (s32[]{:T(128)}, f32[1024,3,64]{0,2,1:T(8,128)S(1)}, f32[1024,3,64]{0,2,1:T(8,128)S(1)}, f32[2,512,3,64]{1,3,2,0:T(8,128)S(1)}, s32[2]{0:T(128)S(1)}...) while((s32[]{:T(128)}, f32[1024,3,64]{0,2,1:T(8,128)S(1)}, ...), condition=%wide.region_40.42_spmd.clone, body=%wide.region_36.41_spmd.clone.sunk | while | flops 5059938816 | bytes 90376584 | solution.py:184
  803.2 63.7 %all-reduce.5.cloned.1.call-done = f32[2,768,768]{1,0,2:T(2,128)} async-done(((f32[2,768,768]{1,0,2:T(2,128)}), f32[2,768,768]{1,0,2:T(2,128)}) %all-reduce.5.cloned.1.call-update) | async-done | bytes 4718608
  869.0 40.8 %all-reduce.1 = (f32[2,768]{1,0:T(2,128)}, f32[2,2,768]{2,1,0:T(2,128)}, f32[2,2,768]{2,1,0:T(2,128)}, f32[2,768]{1,0:T(2,128)}) all-reduce(f32[2,768]{1,0:T(2,128)S(1)} %pad_maximum_fusion.10, f32[2,2,768]{2,1,0:T(2,128)S(1)} %pad_maximum_fusion.8, ...), channel_id=1, replica_groups=mesh['dp'=8,'tensor'=4] {'dp','tensor'}, use_global_device_ids=true, to_apply=%region_51.53 | all-reduce | flops 9216 | bytes 73728 | tf_op jit(solution)/shard_map/psum | solution.py:421
  910.3 36.8 %all-reduce.2 = (f32[2,2,192]{2,1,0:T(2,128)}, f32[2,768]{1,0:T(2,128)}) all-reduce(f32[2,2,192]{2,1,0:T(2,128)S(1)} %pad_maximum_fusion.13, f32[2,768]{1,0:T(2,128)S(1)} %pad_maximum_fusion.11), channel_id=1, replica_groups=mesh['dp'=8,'tensor'=4] {'dp'}, use_global_device_ids=true, to_apply=%region_47.49 | all-reduce | flops 2304 | bytes 18432 | tf_op jit(solution)/shard_map/psum | solution.py:414
  948.9 24.6 %reduce-scatter.30.cloned.1.call-done = f32[256,768]{1,0:T(8,128)} async-done(((f32[1024,768]{1,0:T(8,128)}), f32[256,768]{1,0:T(8,128)}) %reduce-scatter.30.cloned.1.call-update) | async-done | bytes 786448 | tf_op jit(solution)/shard_map/reduce_scatter | solution.py:49
  975.6 80.4 %reduce-scatter.34.cloned.1.call-done = f32[96,1152]{1,0:T(8,128)} async-done(((f32[768,1152]{1,0:T(8,128)}), f32[96,1152]{1,0:T(8,128)}) %reduce-scatter.34.cloned.1.call-update) | async-done | bytes 442384
  1058.6 96.8 %reduce-scatter.32.cloned.1.call-done = f32[2,96,768]{2,1,0:T(8,128)} async-done(((f32[2,768,768]{2,1,0:T(8,128)}), f32[2,96,768]{2,1,0:T(8,128)}) %reduce-scatter.32.cloned.1.call-update) | async-done | bytes 589840 | tf_op jit(solution)/shard_map/reduce_scatter | solution.py:409
  (512 shorter events, 394.7 us)
Async XLA Ops:
  7.2 103.9 %reduce-scatter.16.cloned.1.call-start = ((), (), s32[]{:S(2)}) async-start(), calls=%async_computation.11 | async-start | bytes 3932160 | tf_op jit(solution)/shard_map/reduce_scatter | solution.py:36
  7.2 8.1 collective-permute-start
  16.4 20.4 %collective-permute-start.1 = (bf16[512,768]{1,0:T(8,128)(2,1)S(1)}, bf16[512,768]{1,0:T(8,128)(2,1)}, u32[]{:S(2)}, u32[]{:S(2)}) collective-permute-start(bf16[512,768]{1,0:T(8,128)(2,1)S(1)} %pad_maximum_fusion.4), channel_id=1, source_target_pairs={{0,2},{1,3},{2,0},{3,1},{4,6},{5,7},{6,4},{7,5},{8,10},{9,11},{10,... | collective-permute-start | bytes 2359304 | tf_op jit(solution)/shard_map/ppermute | solution.py:24
  72.7 124.0 %reduce-scatter.18.cloned.1.call-start = ((), (), s32[]{:S(2)}) async-start(), calls=%async_computation.12 | async-start | bytes 3932160 | tf_op jit(solution)/shard_map/reduce_scatter | solution.py:36
  112.9 5.5 collective-permute-start.2
  118.5 19.8 %collective-permute-start.3 = (bf16[512,768]{1,0:T(8,128)(2,1)S(1)}, bf16[512,768]{1,0:T(8,128)(2,1)S(1)}, u32[]{:S(2)}, u32[]{:S(2)}) collective-permute-start(bf16[512,768]{1,0:T(8,128)(2,1)S(1)} %pad_maximum_fusion.5), channel_id=1, source_target_pairs={{0,2},{1,3},{2,0},{3,1},{4,6},{5,7},{6,4},{7,5},{8,10},{9,11},{10,... | collective-permute-start | bytes 2359304 | tf_op jit(solution)/shard_map/ppermute | solution.py:24
  157.1 146.3 %reduce-scatter.20.cloned.1.call-start = ((), (), s32[]{:S(2)}) async-start(), calls=%async_computation.13 | async-start | bytes 3932160 | tf_op jit(solution)/shard_map/reduce_scatter | solution.py:36
  198.7 5.6 collective-permute-start.4
  204.3 19.9 %collective-permute-start.5 = (bf16[512,768]{1,0:T(8,128)(2,1)S(1)}, bf16[512,768]{1,0:T(8,128)(2,1)}, u32[]{:S(2)}, u32[]{:S(2)}) collective-permute-start(bf16[512,768]{1,0:T(8,128)(2,1)S(1)} %pad_maximum_fusion.6), channel_id=1, source_target_pairs={{0,2},{1,3},{2,0},{3,1},{4,6},{5,7},{6,4},{7,5},{8,10},{9,11},{10,... | collective-permute-start | bytes 2359304 | tf_op jit(solution)/shard_map/ppermute | solution.py:24
  263.9 125.4 %reduce-scatter.22.cloned.1.call-start = ((), (), s32[]{:S(2)}) async-start(), calls=%async_computation.14 | async-start | bytes 3932160 | tf_op jit(solution)/shard_map/reduce_scatter | solution.py:36
  305.4 5.8 collective-permute-start.6
  311.2 19.7 %collective-permute-start.7 = (bf16[512,768]{1,0:T(8,128)(2,1)S(1)}, bf16[512,768]{1,0:T(8,128)(2,1)S(1)}, u32[]{:S(2)}, u32[]{:S(2)}) collective-permute-start(bf16[512,768]{1,0:T(8,128)(2,1)S(1)} %pad_maximum_fusion.7), channel_id=1, source_target_pairs={{0,2},{1,3},{2,0},{3,1},{4,6},{5,7},{6,4},{7,5},{8,10},{9,11},{10,... | collective-permute-start | bytes 2359304 | tf_op jit(solution)/shard_map/ppermute | solution.py:24
  349.7 64.7 %all-gather.5.cloned.1.call-start = ((), (), s32[]{:S(2)}) async-start(), calls=%async_computation.15 | async-start | bytes 1966080 | tf_op jit(solution)/shard_map/all_gather | solution.py:45
  394.6 72.0 %reduce-scatter.24.cloned.1.call-start = ((), (), s32[]{:S(2)}) async-start(), calls=%async_computation.16 | async-start | bytes 3932160 | tf_op jit(solution)/shard_map/reduce_scatter | solution.py:49
  428.5 62.7 %all-gather.7.cloned.1.call-start = ((), (), s32[]{:S(2)}) async-start(), calls=%async_computation.17 | async-start | bytes 1966080 | tf_op jit(solution)/shard_map/all_gather | solution.py:45
  471.4 121.5 %reduce-scatter.26.cloned.1.call-start = ((), (), s32[]{:S(2)}) async-start(), calls=%async_computation.18 | async-start | bytes 3932160 | tf_op jit(solution)/shard_map/reduce_scatter | solution.py:49
  554.8 61.8 %all-gather.9.cloned.1.call-start = ((), (), s32[]{:S(2)}) async-start(), calls=%async_computation.19 | async-start | bytes 1966080 | tf_op jit(solution)/shard_map/all_gather | solution.py:45
  596.8 72.0 %reduce-scatter.28.cloned.1.call-start = ((), (), s32[]{:S(2)}) async-start(), calls=%async_computation.20 | async-start | bytes 3932160 | tf_op jit(solution)/shard_map/reduce_scatter | solution.py:49
  630.7 62.7 %all-gather.11.cloned.1.call-start = ((), (), s32[]{:S(2)}) async-start(), calls=%async_computation.21 | async-start | bytes 1966080 | tf_op jit(solution)/shard_map/all_gather | solution.py:45
  673.6 193.4 %all-reduce.5.cloned.1.call-start = ((), (), s32[]{:S(2)}) async-start(), calls=%async_computation.26 | async-start | bytes 9437184
  688.8 258.2 %reduce-scatter.36.cloned.1.call-start = ((), (), s32[]{:S(2)}) async-start(), calls=%async_computation.25 | async-start | bytes 1327104
  701.9 271.6 %reduce-scatter.30.cloned.1.call-start = ((), (), s32[]{:S(2)}) async-start(), calls=%async_computation.22 | async-start | bytes 3932160 | tf_op jit(solution)/shard_map/reduce_scatter | solution.py:49
  764.4 291.7 %reduce-scatter.34.cloned.1.call-start = ((), (), s32[]{:S(2)}) async-start(), calls=%async_computation.24 | async-start | bytes 3981312
  786.3 369.0 %reduce-scatter.32.cloned.1.call-start = ((), (), s32[]{:S(2)}) async-start(), calls=%async_computation.23 | async-start | bytes 5308416 | tf_op jit(solution)/shard_map/reduce_scatter | solution.py:409
  (118 other events, 2549.8 us)
Sparse Core Ops, SparseCore 0:
  72.8 38.2 reduce-scatter.15
  157.2 39.4 reduce-scatter.17
  264.0 39.4 reduce-scatter.19
  349.8 39.4 reduce-scatter.21
  394.7 19.6 all-gather.4
  428.6 37.9 reduce-scatter.23
  471.5 19.6 all-gather.6
  554.9 37.9 reduce-scatter.25
  596.9 19.6 all-gather.8
  630.8 37.9 reduce-scatter.27
  673.7 19.6 all-gather.10
  697.3 169.6 all-reduce.4
  870.7 63.2 reduce-scatter.35
  936.5 36.9 reduce-scatter.29
  977.0 79.0 reduce-scatter.33
  1060.1 95.1 reduce-scatter.31
